TPU v7x, 512 devices: a whole 4x4x16 slice. The times are simulated.
512 devices in a mesh: seq: 128 (over z, y, x_hi), branch: 4 (over x_lo, core).
Axes of the slice: x: 4 (x_hi: 2, x_lo: 2; x = x_hi * 2 + x_lo), y: 4, z: 16, core: 2. Of those that a mesh axis runs over, the one named last changes fastest.
Arguments:
- q_ctl: bfloat16 [4, 24576, 2048], P('branch', 'seq'), may hold values from -64 to 64
- k_ctl: bfloat16 [4, 24576, 2048], P('branch', 'seq'), may hold values from -64 to 64
- v_ctl: bfloat16 [4, 24576, 2048], P('branch', 'seq'), may hold values from -6 to 6
- positions: int32 [24576], P('seq'), may hold values from 0 to 12287
- branch_ids: int32 [4], P('branch'), may hold values from 0 to 63
- cond_scale: float32 [64], replicated, may hold values from 0.25 to 2
- out_weight: bfloat16 [2048, 3072], P('branch', 'seq'), may hold values from -0.125 to 0.125
- frozen: bfloat16 [24576, 3072], P(('seq', 'branch')), may hold values from -2.390625 to 2.390625
- norm_gain: float32 [3072], replicated, may hold values from 0.5 to 1.5
- cotangent: bfloat16 [24576, 3072], P('seq'), may hold values from -6 to 6
Outputs:
- normed: bfloat16 [24576, 3072], P(('seq', 'branch'))
- grad_attn: bfloat16 [4, 24576, 2048], P('branch', 'seq')
All inputs are finite; a program needn't handle non-finite values.
Results may differ from a plain program's by a relative error of at most 0.014.
Values may be sent and summed in bfloat16 or wider, within the bound.
No kernel may reach another device: no remote copies, remote signals or barrier semaphores. Data moves between devices by JAX's collectives and lax.ppermute only.
A program may use at most 64 MiB of HBM per device.

v0:
```python
import math
import jax
import jax.numpy as jnp
from jax import lax
from jax.sharding import PartitionSpec as P

HEADS = 16
HEAD_DIM = 128
EPS = 1e-06


def from_partner(shard, axis, distance):
    return lax.ppermute(shard, axis, [(i, i ^ 1 << distance) for i in range(lax.axis_size(axis))])


def rope_tables(positions, head_dim):
    exponents = jnp.arange(head_dim // 2, dtype=jnp.float32) * (2.0 / head_dim)
    frequencies = 10000.0 ** (-exponents)
    angles = positions.astype(jnp.float32)[..., None] * frequencies
    return (jnp.cos(angles), jnp.sin(angles))


def rotate(values_in, cosines, sines):
    half_dim = values_in.shape[-1] // 2
    front_half = values_in[..., :half_dim]
    back_half = values_in[..., half_dim:]
    return jnp.concatenate(
        [front_half * cosines - back_half * sines, back_half * cosines + front_half * sines],
        axis=-1,
    )


def normalize(hidden, norm_gain):
    inverse = lax.rsqrt(jnp.mean(hidden * hidden, axis=-1, keepdims=True) + EPS)
    return (hidden * inverse * norm_gain).astype(jnp.bfloat16)


def norm_grad(hidden, norm_gain, cotangent):
    inverse = lax.rsqrt(jnp.mean(hidden * hidden, axis=-1, keepdims=True) + EPS)
    upstream = cotangent.astype(jnp.float32) * norm_gain
    inner_mean = jnp.mean(upstream * hidden, axis=-1, keepdims=True)
    return (inverse * upstream - hidden * (inverse * inverse * inverse) * inner_mean).astype(
        jnp.bfloat16
    )


def attend_head(packed):
    query_rows, key_rows, value_rows = packed
    clip_len = query_rows.shape[0]
    block_rows = min(512, clip_len)
    factor = 1.0 / math.sqrt(query_rows.shape[-1])

    def one_block(query_block):
        scores = jnp.dot(query_block, key_rows.T, preferred_element_type=jnp.float32) * factor
        row_max = jnp.max(scores, axis=-1, keepdims=True)
        weights = jnp.exp(scores - row_max)
        row_total = jnp.sum(weights, axis=-1, keepdims=True)
        weights_low = (weights / row_total).astype(jnp.bfloat16)
        return jnp.dot(weights_low, value_rows, preferred_element_type=jnp.float32).astype(
            jnp.bfloat16
        )

    blocks = query_rows.reshape(clip_len // block_rows, block_rows, query_rows.shape[-1])
    return lax.map(one_block, blocks).reshape(clip_len, query_rows.shape[-1])


def regroup(buffer, group_bits, seq_index, forward):
    full_shape = buffer.shape
    split = buffer.reshape(full_shape[:1] + (2,) * group_bits + full_shape[2:])
    for bit in range(group_bits):
        axis_here = group_bits - bit
        mine = jnp.bitwise_and(jnp.right_shift(seq_index, bit), 1)
        other = 1 - mine
        outgoing = lax.dynamic_index_in_dim(split, other, axis_here, keepdims=True)
        if forward:
            incoming = from_partner(outgoing, "seq", bit)
        else:
            incoming = from_partner(outgoing, "seq", bit)
        split = lax.dynamic_update_index_in_dim(split, incoming, other, axis_here)
    return split.reshape(full_shape)


def on_device(
    q_ctl, k_ctl, v_ctl, positions, branch_ids, cond_scale, out_weight, frozen, norm_gain, cotangent
):
    branch_index = lax.axis_index("branch")
    quarters = lax.axis_size("branch")
    seq_index = lax.axis_index("seq")
    seq_devices = lax.axis_size("seq")
    group = min(HEADS, seq_devices)
    group_bits = group.bit_length() - 1
    local_len = q_ctl.shape[1]
    feature_width = q_ctl.shape[2]
    head_dim = HEAD_DIM
    head_count = feature_width // head_dim
    heads_here = head_count // group
    clip_len = group * local_len
    quarter_len = local_len // quarters
    model_width = cotangent.shape[1]
    cosines, sines = rope_tables(positions, head_dim)
    cosines = cosines[:, None, :]
    sines = sines[:, None, :]

    def heads_first(source, rotated):
        split_heads = source[0].reshape(local_len, head_count, head_dim)
        if rotated:
            split_heads = rotate(split_heads.astype(jnp.float32), cosines, sines).astype(
                jnp.bfloat16
            )
        split_heads = split_heads.reshape(local_len, group, heads_here, head_dim)
        return jnp.transpose(split_heads, (1, 0, 2, 3))

    stacked = jnp.stack(
        [heads_first(q_ctl, True), heads_first(k_ctl, True), heads_first(v_ctl, False)]
    )
    arrived = regroup(stacked, group_bits, seq_index, True)

    def per_head(member):
        return jnp.transpose(member, (2, 0, 1, 3)).reshape(heads_here, clip_len, head_dim)

    attended_heads = lax.map(
        attend_head, (per_head(arrived[0]), per_head(arrived[1]), per_head(arrived[2]))
    )
    going_back = jnp.transpose(
        attended_heads.reshape(heads_here, group, local_len, head_dim), (1, 2, 0, 3)
    )[None]
    returned = regroup(going_back, group_bits, seq_index, False)[0]
    attended = jnp.transpose(returned, (1, 0, 2, 3)).reshape(local_len, feature_width)
    branch_scale = jnp.sum(
        jnp.where(jnp.arange(cond_scale.shape[0]) == branch_ids[0], cond_scale, 0.0)
    )
    weight_rows = lax.all_gather(out_weight, "seq", axis=1, tiled=True)
    mixed = lax.psum_scatter(
        (branch_scale * attended.astype(jnp.float32)).astype(jnp.bfloat16),
        "branch",
        scatter_dimension=1,
        tiled=True,
    ).astype(jnp.float32)
    mixed_high = mixed.astype(jnp.bfloat16)
    mixed_rest = (mixed - mixed_high.astype(jnp.float32)).astype(jnp.bfloat16)
    partial_stream = jnp.dot(mixed_high, weight_rows, preferred_element_type=jnp.float32)
    partial_stream = partial_stream + jnp.dot(
        mixed_rest, weight_rows, preferred_element_type=jnp.float32
    )
    owner = (jnp.arange(quarters) == branch_index).astype(jnp.float32)[:, None, None]
    term = (
        partial_stream.reshape(quarters, quarter_len, model_width)
        + owner * frozen.astype(jnp.float32)[None]
    )
    hidden = (
        lax.psum(term.astype(jnp.bfloat16), "branch")
        .astype(jnp.float32)
        .reshape(local_len, model_width)
    )
    hidden_share = lax.dynamic_slice_in_dim(hidden, branch_index * quarter_len, quarter_len, 0)
    normed = normalize(hidden_share, norm_gain)
    grad_hidden = norm_grad(hidden, norm_gain, cotangent)
    cot_block = jnp.einsum(
        "td,hd->th", grad_hidden, weight_rows, preferred_element_type=jnp.float32
    ).astype(jnp.bfloat16)
    cot_attn = lax.all_gather(cot_block, "branch", axis=1, tiled=True)
    grad_attn = (branch_scale * cot_attn.astype(jnp.float32)).astype(jnp.bfloat16)
    return (normed, grad_attn.reshape(1, local_len, feature_width))


def solution(mesh):
    return jax.shard_map(
        on_device,
        mesh=mesh,
        in_specs=(
            P("branch", "seq", None),
            P("branch", "seq", None),
            P("branch", "seq", None),
            P("seq"),
            P("branch"),
            P(),
            P("branch", "seq"),
            P(("seq", "branch"), None),
            P(),
            P("seq", None),
        ),
        out_specs=(P(("seq", "branch"), None), P("branch", "seq", None)),
        check_vma=False,
    )
```

profile of v0, /device:TPU:1, one launch (start us, length us, event | category | flops | bytes accessed | tf_op | source)
XLA Modules:
  0.0 424.5 jit_solution(8821610244191821590)
XLA Ops:
  8.7 1.4 convert_bitcast_fusion.1
  15.9 1.6 pad_maximum_fusion
  18.6 5.4 %collective-permute-start = (bf16[3,2,2,2,1,192,1,128]{7,5,4,3,2,1,6,0:T(8,128)(2,1)}, bf16[3,2,2,2,1,192,1,128]{7,5,4,3,2,1,6,0:T(8,128)(2,1)S(1)}, u32[]{:S(2)}, u32[]{:S(2)}) collective-permute-start(bf16[3,2,2,2,1,192,1,128]{7,5,4,3,2,1,6,0:T(8,128)(2,1)} %constant_dynamic-slice_fusion.7), channel_id=1, source_target_pairs={{0,4},{4,0},{8,12},{12,8},{16,20},{20,16},{24,28},{28,24},{32,36},... | collective-permute-start | bytes 3538952 | tf_op jit(solution)/shard_map/ppermute | solution.py:13
  24.1 22.6 %collective-permute-done = bf16[3,2,2,2,1,192,1,128]{7,5,4,3,2,1,6,0:T(8,128)(2,1)S(1)} collective-permute-done((bf16[3,2,2,2,1,192,1,128]{7,5,4,3,2,1,6,0:T(8,128)(2,1)}, bf16[3,2,2,2,1,192,1,128]{7,5,4,3,2,1,6,0:T(8,128)(2,1)S(1)}, u32[]{:S(2)}, u32[]{:S(2)}) %collective-permute-start) | collective-permute-done | bytes 1179680 | tf_op jit(solution)/shard_map/ppermute | solution.py:13
  47.9 6.5 %collective-permute-start.1 = (bf16[3,2,2,1,2,192,1,128]{7,5,4,3,2,1,6,0:T(8,128)(2,1)}, bf16[3,2,2,1,2,192,1,128]{7,5,4,3,2,1,6,0:T(8,128)(2,1)S(1)}, u32[]{:S(2)}, u32[]{:S(2)}) collective-permute-start(bf16[3,2,2,1,2,192,1,128]{7,5,4,3,2,1,6,0:T(8,128)(2,1)} %constant_dynamic-slice_fusion.6), channel_id=1, source_target_pairs={{0,8},{4,12},{8,0},{12,4},{16,24},{20,28},{24,16},{28,20},{32,40},... | collective-permute-start | bytes 3538952 | tf_op jit(solution)/shard_map/ppermute | solution.py:13
  54.4 24.8 %collective-permute-done.1 = bf16[3,2,2,1,2,192,1,128]{7,5,4,3,2,1,6,0:T(8,128)(2,1)S(1)} collective-permute-done((bf16[3,2,2,1,2,192,1,128]{7,5,4,3,2,1,6,0:T(8,128)(2,1)}, bf16[3,2,2,1,2,192,1,128]{7,5,4,3,2,1,6,0:T(8,128)(2,1)S(1)}, u32[]{:S(2)}, u32[]{:S(2)}) %collective-permute-start.1) | collective-permute-done | bytes 1179680 | tf_op jit(solution)/shard_map/ppermute | solution.py:13
  80.5 4.9 %collective-permute-start.2 = (bf16[3,2,1,2,2,192,1,128]{7,5,4,3,2,1,6,0:T(8,128)(2,1)}, bf16[3,2,1,2,2,192,1,128]{7,5,4,3,2,1,6,0:T(8,128)(2,1)S(1)}, u32[]{:S(2)}, u32[]{:S(2)}) collective-permute-start(bf16[3,2,1,2,2,192,1,128]{7,5,4,3,2,1,6,0:T(8,128)(2,1)} %constant_dynamic-slice_fusion.5), channel_id=1, source_target_pairs={{0,16},{4,20},{8,24},{12,28},{16,0},{20,4},{24,8},{28,12},{32,48},... | collective-permute-start | bytes 3538952 | tf_op jit(solution)/shard_map/ppermute | solution.py:13
  85.4 24.0 %collective-permute-done.2 = bf16[3,2,1,2,2,192,1,128]{7,5,4,3,2,1,6,0:T(8,128)(2,1)S(1)} collective-permute-done((bf16[3,2,1,2,2,192,1,128]{7,5,4,3,2,1,6,0:T(8,128)(2,1)}, bf16[3,2,1,2,2,192,1,128]{7,5,4,3,2,1,6,0:T(8,128)(2,1)S(1)}, u32[]{:S(2)}, u32[]{:S(2)}) %collective-permute-start.2) | collective-permute-done | bytes 1179680 | tf_op jit(solution)/shard_map/ppermute | solution.py:13
  110.8 3.5 collective-permute-start.3
  114.3 23.2 %collective-permute-done.3 = bf16[3,1,2,2,2,192,1,128]{7,5,4,3,2,1,6,0:T(8,128)(2,1)S(1)} collective-permute-done((bf16[3,1,2,2,2,192,1,128]{7,5,4,3,2,1,6,0:T(8,128)(2,1)}, bf16[3,1,2,2,2,192,1,128]{7,5,4,3,2,1,6,0:T(8,128)(2,1)S(1)}, u32[]{:S(2)}, u32[]{:S(2)}) %collective-permute-start.3) | collective-permute-done | bytes 1179680 | tf_op jit(solution)/shard_map/ppermute | solution.py:13
  137.7 1.4 fusion.22
  139.0 31.2 %while.17 = (s32[]{:T(128)}, bf16[6,512,128]{2,1,0:T(8,128)(2,1)}, bf16[6,512,128]{2,1,0:T(8,128)(2,1)}, bf16[3072,128]{1,0:T(8,128)(2,1)S(1)}, bf16[3072,128]{1,0:T(8,128)(2,1)}, /*index=5*/s32[]{:T(128)}) while((s32[]{:T(128)}, bf16[6,512,128]{2,1,0:T(8,128)(2,1)}, bf16[6,512,128]{2,1,0:T(8,128)(2,1)}, bf16[3072,128]{1,0:T(8,128)(2,1)S(1)}, ...), condition=%wide.region_4.5_spmd, body=%wide.region_1.4_spmd.sunk | while | flops 819526656 | bytes 23866464 | solution.py:64
  139.0 2.0 multiply_reduce_fusion.5
  141.0 1.2 fusion.36
  142.2 2.1 fusion.37
  144.2 2.0 multiply_reduce_fusion.5
  146.2 1.2 fusion.36
  147.4 2.1 fusion.37
  149.4 2.0 multiply_reduce_fusion.5
  151.4 1.2 fusion.36
  152.6 2.1 fusion.37
  154.6 2.0 multiply_reduce_fusion.5
  156.6 1.2 fusion.36
  157.8 2.1 fusion.37
  159.8 2.0 multiply_reduce_fusion.5
  161.8 1.2 fusion.36
  163.0 2.1 fusion.37
  165.0 2.0 multiply_reduce_fusion.5
  167.0 1.2 fusion.36
  168.2 2.1 fusion.37
  171.3 4.6 %collective-permute-start.4 = (bf16[1,2,2,2,1,192,1,128]{7,5,4,3,2,1,6,0:T(8,128)(2,1)S(1)}, bf16[1,2,2,2,1,192,1,128]{7,5,4,3,2,1,6,0:T(8,128)(2,1)S(1)}, u32[]{:S(2)}, u32[]{:S(2)}) collective-permute-start(bf16[1,2,2,2,1,192,1,128]{7,5,4,3,2,1,6,0:T(8,128)(2,1)S(1)} %constant_dynamic-slice_fusion.3), channel_id=1, source_target_pairs={{0,4},{4,0},{8,12},{12,8},{16,20},{20,16},{24,28},{28,24},{32,36},... | collective-permute-start | bytes 1179656 | tf_op jit(solution)/shard_map/ppermute | solution.py:13
  175.9 5.4 %collective-permute-done.4 = bf16[1,2,2,2,1,192,1,128]{7,5,4,3,2,1,6,0:T(8,128)(2,1)S(1)} collective-permute-done((bf16[1,2,2,2,1,192,1,128]{7,5,4,3,2,1,6,0:T(8,128)(2,1)S(1)}, bf16[1,2,2,2,1,192,1,128]{7,5,4,3,2,1,6,0:T(8,128)(2,1)S(1)}, u32[]{:S(2)}, u32[]{:S(2)}) %collective-permute-start.4) | collective-permute-done | bytes 393248 | tf_op jit(solution)/shard_map/ppermute | solution.py:13
  183.2 3.2 collective-permute-start.5
  186.3 5.7 %collective-permute-done.5 = bf16[1,2,2,1,2,192,1,128]{7,5,4,3,2,1,6,0:T(8,128)(2,1)S(1)} collective-permute-done((bf16[1,2,2,1,2,192,1,128]{7,5,4,3,2,1,6,0:T(8,128)(2,1)S(1)}, bf16[1,2,2,1,2,192,1,128]{7,5,4,3,2,1,6,0:T(8,128)(2,1)S(1)}, u32[]{:S(2)}, u32[]{:S(2)}) %collective-permute-start.5) | collective-permute-done | bytes 393248 | tf_op jit(solution)/shard_map/ppermute | solution.py:13
  193.9 4.8 %collective-permute-start.6 = (bf16[1,2,1,2,2,192,1,128]{7,5,4,3,2,1,6,0:T(8,128)(2,1)S(1)}, bf16[1,2,1,2,2,192,1,128]{7,5,4,3,2,1,6,0:T(8,128)(2,1)S(1)}, u32[]{:S(2)}, u32[]{:S(2)}) collective-permute-start(bf16[1,2,1,2,2,192,1,128]{7,5,4,3,2,1,6,0:T(8,128)(2,1)S(1)} %constant_dynamic-slice_fusion.1), channel_id=1, source_target_pairs={{0,16},{4,20},{8,24},{12,28},{16,0},{20,4},{24,8},{28,12},{32,48},... | collective-permute-start | bytes 1179656 | tf_op jit(solution)/shard_map/ppermute | solution.py:13
  198.7 5.2 %collective-permute-done.6 = bf16[1,2,1,2,2,192,1,128]{7,5,4,3,2,1,6,0:T(8,128)(2,1)S(1)} collective-permute-done((bf16[1,2,1,2,2,192,1,128]{7,5,4,3,2,1,6,0:T(8,128)(2,1)S(1)}, bf16[1,2,1,2,2,192,1,128]{7,5,4,3,2,1,6,0:T(8,128)(2,1)S(1)}, u32[]{:S(2)}, u32[]{:S(2)}) %collective-permute-start.6) | collective-permute-done | bytes 393248 | tf_op jit(solution)/shard_map/ppermute | solution.py:13
  205.8 3.5 collective-permute-start.7
  210.6 4.3 %collective-permute-done.7 = bf16[1,1,2,2,2,192,1,128]{7,5,4,3,2,1,6,0:T(8,128)(2,1)S(1)} collective-permute-done((bf16[1,1,2,2,2,192,1,128]{7,5,4,3,2,1,6,0:T(8,128)(2,1)S(1)}, bf16[1,1,2,2,2,192,1,128]{7,5,4,3,2,1,6,0:T(8,128)(2,1)S(1)}, u32[]{:S(2)}, u32[]{:S(2)}) %collective-permute-start.7) | collective-permute-done | bytes 393248 | tf_op jit(solution)/shard_map/ppermute | solution.py:13
  215.6 2.0 multiply_convert_fusion.1
  220.4 109.9 %all-gather.2.cloned.1.call-done = bf16[512,3072]{0,1:T(8,128)(2,1)} async-done(((bf16[512,24]{0,1:T(8,128)(2,1)}), bf16[512,3072]{0,1:T(8,128)(2,1)}) %all-gather.2.cloned.1.call-update) | async-done | bytes 3145744 | tf_op jit(solution)/shard_map/all_gather | solution.py:132
  330.4 3.3 fusion.23
  333.7 1.2 convolution_add_fusion
  334.9 1.3 add_convert_fusion
  336.3 62.4 %all-reduce.2.cloned.1.call-done = bf16[4,48,3072]{2,1,0:T(8,128)(2,1)} async-done(((bf16[4,48,3072]{2,1,0:T(8,128)(2,1)}), bf16[4,48,3072]{2,1,0:T(8,128)(2,1)}) %all-reduce.2.cloned.1.call-update) | async-done | bytes 1179664 | tf_op jit(solution)/shard_map/psum | solution.py:151
  398.7 3.5 multiply_reduce_fusion.1
  402.7 2.8 fusion.15
  405.5 8.8 %all_gather.7 = bf16[192,2048]{1,0:T(8,128)(2,1)S(1)} all-gather(bf16[192,512]{1,0:T(8,128)(2,1)S(1)} %fusion.15), channel_id=1, replica_groups=mesh['seq'=128,'branch'=4] {'branch'}, dimensions={1}, use_global_device_ids=true | all-gather | bytes 983040 | tf_op jit(solution)/shard_map/all_gather | solution.py:161
  414.4 1.7 fusion.20
  (81 shorter events, 24.0 us)
Async XLA Ops:
  8.0 322.4 %all-gather.2.cloned.1.call-start = ((), (), s32[]{:S(2)}) async-start(), calls=%async_computation.2 | async-start | bytes 3170304 | tf_op jit(solution)/shard_map/all_gather | solution.py:132
  8.7 1.7 copy-start.7
  13.3 1.3 copy-start.6
  18.6 28.0 %collective-permute-start = (bf16[3,2,2,2,1,192,1,128]{7,5,4,3,2,1,6,0:T(8,128)(2,1)}, bf16[3,2,2,2,1,192,1,128]{7,5,4,3,2,1,6,0:T(8,128)(2,1)S(1)}, u32[]{:S(2)}, u32[]{:S(2)}) collective-permute-start(bf16[3,2,2,2,1,192,1,128]{7,5,4,3,2,1,6,0:T(8,128)(2,1)} %constant_dynamic-slice_fusion.7), channel_id=1, source_target_pairs={{0,4},{4,0},{8,12},{12,8},{16,20},{20,16},{24,28},{28,24},{32,36},... | collective-permute-start | bytes 3538952 | tf_op jit(solution)/shard_map/ppermute | solution.py:13
  47.9 31.3 %collective-permute-start.1 = (bf16[3,2,2,1,2,192,1,128]{7,5,4,3,2,1,6,0:T(8,128)(2,1)}, bf16[3,2,2,1,2,192,1,128]{7,5,4,3,2,1,6,0:T(8,128)(2,1)S(1)}, u32[]{:S(2)}, u32[]{:S(2)}) collective-permute-start(bf16[3,2,2,1,2,192,1,128]{7,5,4,3,2,1,6,0:T(8,128)(2,1)} %constant_dynamic-slice_fusion.6), channel_id=1, source_target_pairs={{0,8},{4,12},{8,0},{12,4},{16,24},{20,28},{24,16},{28,20},{32,40},... | collective-permute-start | bytes 3538952 | tf_op jit(solution)/shard_map/ppermute | solution.py:13
  80.5 28.9 %collective-permute-start.2 = (bf16[3,2,1,2,2,192,1,128]{7,5,4,3,2,1,6,0:T(8,128)(2,1)}, bf16[3,2,1,2,2,192,1,128]{7,5,4,3,2,1,6,0:T(8,128)(2,1)S(1)}, u32[]{:S(2)}, u32[]{:S(2)}) collective-permute-start(bf16[3,2,1,2,2,192,1,128]{7,5,4,3,2,1,6,0:T(8,128)(2,1)} %constant_dynamic-slice_fusion.5), channel_id=1, source_target_pairs={{0,16},{4,20},{8,24},{12,28},{16,0},{20,4},{24,8},{28,12},{32,48},... | collective-permute-start | bytes 3538952 | tf_op jit(solution)/shard_map/ppermute | solution.py:13
  110.8 26.7 %collective-permute-start.3 = (bf16[3,1,2,2,2,192,1,128]{7,5,4,3,2,1,6,0:T(8,128)(2,1)}, bf16[3,1,2,2,2,192,1,128]{7,5,4,3,2,1,6,0:T(8,128)(2,1)S(1)}, u32[]{:S(2)}, u32[]{:S(2)}) collective-permute-start(bf16[3,1,2,2,2,192,1,128]{7,5,4,3,2,1,6,0:T(8,128)(2,1)} %constant_dynamic-slice_fusion.4), channel_id=1, source_target_pairs={{0,32},{4,36},{8,40},{12,44},{16,48},{20,52},{24,56},{28,60},{32,0... | collective-permute-start | bytes 3538952 | tf_op jit(solution)/shard_map/ppermute | solution.py:13
  114.3 216.1 %reduce-scatter.2.cloned.1.call-start = ((), (), s32[]{:S(2)}) async-start(), calls=%async_computation.1 | async-start | bytes 983040 | tf_op jit(solution)/shard_map/reduce_scatter | solution.py:133
  141.0 1.2 copy-start.4
  146.2 1.2 copy-start.4
  151.4 1.2 copy-start.4
  156.6 1.2 copy-start.4
  161.8 1.2 copy-start.4
  167.0 1.2 copy-start.4
  171.3 38.6 %copy-start.10 = (f32[64]{0:T(128)S(1)}, f32[64]{0:T(128)}, u32[]{:S(2)}) copy-start(f32[64]{0:T(128)} %param.17) | copy-start | bytes 772
  171.3 10.0 %collective-permute-start.4 = (bf16[1,2,2,2,1,192,1,128]{7,5,4,3,2,1,6,0:T(8,128)(2,1)S(1)}, bf16[1,2,2,2,1,192,1,128]{7,5,4,3,2,1,6,0:T(8,128)(2,1)S(1)}, u32[]{:S(2)}, u32[]{:S(2)}) collective-permute-start(bf16[1,2,2,2,1,192,1,128]{7,5,4,3,2,1,6,0:T(8,128)(2,1)S(1)} %constant_dynamic-slice_fusion.3), channel_id=1, source_target_pairs={{0,4},{4,0},{8,12},{12,8},{16,20},{20,16},{24,28},{28,24},{32,36},... | collective-permute-start | bytes 1179656 | tf_op jit(solution)/shard_map/ppermute | solution.py:13
  183.2 8.9 %collective-permute-start.5 = (bf16[1,2,2,1,2,192,1,128]{7,5,4,3,2,1,6,0:T(8,128)(2,1)S(1)}, bf16[1,2,2,1,2,192,1,128]{7,5,4,3,2,1,6,0:T(8,128)(2,1)S(1)}, u32[]{:S(2)}, u32[]{:S(2)}) collective-permute-start(bf16[1,2,2,1,2,192,1,128]{7,5,4,3,2,1,6,0:T(8,128)(2,1)S(1)} %constant_dynamic-slice_fusion.2), channel_id=1, source_target_pairs={{0,8},{4,12},{8,0},{12,4},{16,24},{20,28},{24,16},{28,20},{32,40},... | collective-permute-start | bytes 1179656 | tf_op jit(solution)/shard_map/ppermute | solution.py:13
  193.9 10.0 %collective-permute-start.6 = (bf16[1,2,1,2,2,192,1,128]{7,5,4,3,2,1,6,0:T(8,128)(2,1)S(1)}, bf16[1,2,1,2,2,192,1,128]{7,5,4,3,2,1,6,0:T(8,128)(2,1)S(1)}, u32[]{:S(2)}, u32[]{:S(2)}) collective-permute-start(bf16[1,2,1,2,2,192,1,128]{7,5,4,3,2,1,6,0:T(8,128)(2,1)S(1)} %constant_dynamic-slice_fusion.1), channel_id=1, source_target_pairs={{0,16},{4,20},{8,24},{12,28},{16,0},{20,4},{24,8},{28,12},{32,48},... | collective-permute-start | bytes 1179656 | tf_op jit(solution)/shard_map/ppermute | solution.py:13
  205.8 9.1 %collective-permute-start.7 = (bf16[1,1,2,2,2,192,1,128]{7,5,4,3,2,1,6,0:T(8,128)(2,1)S(1)}, bf16[1,1,2,2,2,192,1,128]{7,5,4,3,2,1,6,0:T(8,128)(2,1)S(1)}, u32[]{:S(2)}, u32[]{:S(2)}) collective-permute-start(bf16[1,1,2,2,2,192,1,128]{7,5,4,3,2,1,6,0:T(8,128)(2,1)S(1)} %constant_dynamic-slice_fusion), channel_id=1, source_target_pairs={{0,32},{4,36},{8,40},{12,44},{16,48},{20,52},{24,56},{28,60},{32,0... | collective-permute-start | bytes 1179656 | tf_op jit(solution)/shard_map/ppermute | solution.py:13
  217.6 2.0 copy-start.8
  219.5 179.2 %all-reduce.2.cloned.1.call-start = ((), (), s32[]{:S(2)}) async-start(), calls=%async_computation.3 | async-start | bytes 2359296 | tf_op jit(solution)/shard_map/psum | solution.py:151
  330.4 3.3 copy-start
  330.4 3.3 copy-start.5
  333.7 1.2 copy-start.3
  334.9 63.8 %copy-start.9 = (f32[3072]{0:T(1024)S(1)}, f32[3072]{0:T(1024)}, u32[]{:S(2)}) copy-start(f32[3072]{0:T(1024)} %param.20) | copy-start | bytes 36868
  398.7 3.5 copy-start.2
  405.5 10.5 %copy-start.1 = (f32[192,3072]{1,0:T(8,128)S(1)}, f32[192,3072]{1,0:T(8,128)}, u32[]{:S(2)}) copy-start(f32[192,3072]{1,0:T(8,128)} %get-tuple-element.56) | copy-start | bytes 7077892
Sparse Core Ops, SparseCore 0:
  114.4 215.9 all-gather.1
Sparse Core Ops, SparseCore 1:
  219.6 39.7 reduce-scatter.1
  336.4 62.3 all-reduce.1
where the time goes:
time: 425 us; the launch traced here: 424 us
  waiting for transfers between devices  288 us (68%)
  starting transfers between devices  36.4 us (9%)
  matrix products  31.5 us (7%)
  other arithmetic  24.5 us (6%)
  local copies, waits for them, and re-layouts  19.1 us (4%)
  between operations  16.5 us (4%)
  blocking collectives  8.84 us (2%)
    ppermute x8, waiting for transfers between devices, from_partner(): lax.ppermute(shard, axis, [(i, i ^ 1 << distance) for i in range(lax.axis...  115 us
    all_gather x1, waiting for transfers between devices, on_device(): weight_rows = lax.all_gather(out_weight, 'seq', axis=1, tiled=True)  110 us
    psum x1, waiting for transfers between devices, on_device(): lax.psum(term.astype(jnp.bfloat16), 'branch').astype(jnp.float32)  62.4 us
    ppermute x8, starting transfers between devices, from_partner(): lax.ppermute(shard, axis, [(i, i ^ 1 << distance) for i in range(lax.axis...  36.3 us
    dot_general x6, matrix products, one_block(): jnp.dot(weights_low, value_rows, preferred_element_type=jnp.float32)  12.4 us
    dot_general x6, matrix products, one_block(): jnp.dot(query_block, key_rows.T, preferred_element_type=jnp.float32)  11.8 us
    all_gather x1, blocking collectives, on_device(): cot_attn = lax.all_gather(cot_block, 'branch', axis=1, tiled=True)  8.84 us
    dynamic_slice x8, local copies, waits for them, and re-layouts, regroup(): outgoing = lax.dynamic_index_in_dim(split, other, axis_here, keepdims=True)  8.65 us
  transfers between devices with their start and end apart: 11, of which 10 were waited for; matrix products, arithmetic and copies ran while one was open for 11% of the time, Pallas kernels for 0%

commit v1 on v0

--- a/solution.py
+++ b/solution.py
@@ -7,6 +7,7 @@
 HEADS = 16
 HEAD_DIM = 128
 EPS = 1e-06
+tell_copies_now = lambda q_in: jnp.sum(lax.all_gather(q_in, "branch"), 0)
 
 
 def from_partner(shard, axis, distance):
@@ -148,7 +149,7 @@
         + owner * frozen.astype(jnp.float32)[None]
     )
     hidden = (
-        lax.psum(term.astype(jnp.bfloat16), "branch")
+        tell_copies_now(term.astype(jnp.bfloat16))
         .astype(jnp.float32)
         .reshape(local_len, model_width)
     )

time: 425 us -> 432 us (1.016)
  other arithmetic: 24.5 us -> 30.5 us
    all_gather x0 -> x1, waiting for transfers between devices: none -> 63 us  [tell_copies_now = lambda q_in: jnp.sum(lax.all_gather(q_in, 'branch'), 0)]
    psum x1 -> x0, waiting for transfers between devices: 62.4 us -> none  [on_device(): lax.psum(term.astype(jnp.bfloat16), 'branch').astype(jnp.float32)]
    reduce_sum x0 -> x1, other arithmetic: none -> 4.62 us  [tell_copies_now = lambda q_in: jnp.sum(lax.all_gather(q_in, 'branch'), 0)]
where the time goes in v1:
time: 432 us; the launch traced here: 431 us
  waiting for transfers between devices  288 us (67%)
  starting transfers between devices  36.4 us (8%)
  matrix products  31.5 us (7%)
  other arithmetic  30.5 us (7%)
  local copies, waits for them, and re-layouts  19.1 us (4%)
  between operations  16.5 us (4%)
  blocking collectives  8.59 us (2%)
    ppermute x8, waiting for transfers between devices, from_partner(): lax.ppermute(shard, axis, [(i, i ^ 1 << distance) for i in range(lax.axis...  115 us
    all_gather x1, waiting for transfers between devices, on_device(): weight_rows = lax.all_gather(out_weight, 'seq', axis=1, tiled=True)  110 us
    all_gather x1, waiting for transfers between devices, tell_copies_now = lambda q_in: jnp.sum(lax.all_gather(q_in, 'branch'), 0)  63 us
    ppermute x8, starting transfers between devices, from_partner(): lax.ppermute(shard, axis, [(i, i ^ 1 << distance) for i in range(lax.axis...  36.2 us
    dot_general x6, matrix products, one_block(): jnp.dot(weights_low, value_rows, preferred_element_type=jnp.float32)  12.4 us
    dot_general x6, matrix products, one_block(): jnp.dot(query_block, key_rows.T, preferred_element_type=jnp.float32)  11.8 us
    dynamic_slice x8, local copies, waits for them, and re-layouts, regroup(): outgoing = lax.dynamic_index_in_dim(split, other, axis_here, keepdims=True)  8.66 us
  transfers between devices with their start and end apart: 11, of which 10 were waited for; matrix products, arithmetic and copies ran while one was open for 11% of the time, Pallas kernels for 0%

profile of v1, /device:TPU:1, one launch (start us, length us, event | category | flops | bytes accessed | tf_op | source)
XLA Modules:
  0.0 430.7 jit_solution(11873562043466279211)
XLA Ops:
  8.7 1.4 convert_bitcast_fusion.1
  15.8 1.6 pad_maximum_fusion
  18.6 5.4 %collective-permute-start = (bf16[3,2,2,2,1,192,1,128]{7,5,4,3,2,1,6,0:T(8,128)(2,1)}, bf16[3,2,2,2,1,192,1,128]{7,5,4,3,2,1,6,0:T(8,128)(2,1)S(1)}, u32[]{:S(2)}, u32[]{:S(2)}) collective-permute-start(bf16[3,2,2,2,1,192,1,128]{7,5,4,3,2,1,6,0:T(8,128)(2,1)} %constant_dynamic-slice_fusion.7), channel_id=1, source_target_pairs={{0,4},{4,0},{8,12},{12,8},{16,20},{20,16},{24,28},{28,24},{32,36},... | collective-permute-start | bytes 3538952 | tf_op jit(solution)/shard_map/ppermute | solution.py:14
  24.0 22.6 %collective-permute-done = bf16[3,2,2,2,1,192,1,128]{7,5,4,3,2,1,6,0:T(8,128)(2,1)S(1)} collective-permute-done((bf16[3,2,2,2,1,192,1,128]{7,5,4,3,2,1,6,0:T(8,128)(2,1)}, bf16[3,2,2,2,1,192,1,128]{7,5,4,3,2,1,6,0:T(8,128)(2,1)S(1)}, u32[]{:S(2)}, u32[]{:S(2)}) %collective-permute-start) | collective-permute-done | bytes 1179680 | tf_op jit(solution)/shard_map/ppermute | solution.py:14
  47.9 6.5 %collective-permute-start.1 = (bf16[3,2,2,1,2,192,1,128]{7,5,4,3,2,1,6,0:T(8,128)(2,1)}, bf16[3,2,2,1,2,192,1,128]{7,5,4,3,2,1,6,0:T(8,128)(2,1)S(1)}, u32[]{:S(2)}, u32[]{:S(2)}) collective-permute-start(bf16[3,2,2,1,2,192,1,128]{7,5,4,3,2,1,6,0:T(8,128)(2,1)} %constant_dynamic-slice_fusion.6), channel_id=1, source_target_pairs={{0,8},{4,12},{8,0},{12,4},{16,24},{20,28},{24,16},{28,20},{32,40},... | collective-permute-start | bytes 3538952 | tf_op jit(solution)/shard_map/ppermute | solution.py:14
  54.4 24.8 %collective-permute-done.1 = bf16[3,2,2,1,2,192,1,128]{7,5,4,3,2,1,6,0:T(8,128)(2,1)S(1)} collective-permute-done((bf16[3,2,2,1,2,192,1,128]{7,5,4,3,2,1,6,0:T(8,128)(2,1)}, bf16[3,2,2,1,2,192,1,128]{7,5,4,3,2,1,6,0:T(8,128)(2,1)S(1)}, u32[]{:S(2)}, u32[]{:S(2)}) %collective-permute-start.1) | collective-permute-done | bytes 1179680 | tf_op jit(solution)/shard_map/ppermute | solution.py:14
  80.5 4.9 %collective-permute-start.2 = (bf16[3,2,1,2,2,192,1,128]{7,5,4,3,2,1,6,0:T(8,128)(2,1)}, bf16[3,2,1,2,2,192,1,128]{7,5,4,3,2,1,6,0:T(8,128)(2,1)S(1)}, u32[]{:S(2)}, u32[]{:S(2)}) collective-permute-start(bf16[3,2,1,2,2,192,1,128]{7,5,4,3,2,1,6,0:T(8,128)(2,1)} %constant_dynamic-slice_fusion.5), channel_id=1, source_target_pairs={{0,16},{4,20},{8,24},{12,28},{16,0},{20,4},{24,8},{28,12},{32,48},... | collective-permute-start | bytes 3538952 | tf_op jit(solution)/shard_map/ppermute | solution.py:14
  85.4 24.0 %collective-permute-done.2 = bf16[3,2,1,2,2,192,1,128]{7,5,4,3,2,1,6,0:T(8,128)(2,1)S(1)} collective-permute-done((bf16[3,2,1,2,2,192,1,128]{7,5,4,3,2,1,6,0:T(8,128)(2,1)}, bf16[3,2,1,2,2,192,1,128]{7,5,4,3,2,1,6,0:T(8,128)(2,1)S(1)}, u32[]{:S(2)}, u32[]{:S(2)}) %collective-permute-start.2) | collective-permute-done | bytes 1179680 | tf_op jit(solution)/shard_map/ppermute | solution.py:14
  109.6 1.2 constant_dynamic-slice_fusion.4
  110.8 3.5 collective-permute-start.3
  114.3 23.2 %collective-permute-done.3 = bf16[3,1,2,2,2,192,1,128]{7,5,4,3,2,1,6,0:T(8,128)(2,1)S(1)} collective-permute-done((bf16[3,1,2,2,2,192,1,128]{7,5,4,3,2,1,6,0:T(8,128)(2,1)}, bf16[3,1,2,2,2,192,1,128]{7,5,4,3,2,1,6,0:T(8,128)(2,1)S(1)}, u32[]{:S(2)}, u32[]{:S(2)}) %collective-permute-start.3) | collective-permute-done | bytes 1179680 | tf_op jit(solution)/shard_map/ppermute | solution.py:14
  137.7 1.4 fusion.22
  139.0 31.2 %while.17 = (s32[]{:T(128)}, bf16[6,512,128]{2,1,0:T(8,128)(2,1)}, bf16[6,512,128]{2,1,0:T(8,128)(2,1)}, bf16[3072,128]{1,0:T(8,128)(2,1)S(1)}, bf16[3072,128]{1,0:T(8,128)(2,1)}, /*index=5*/s32[]{:T(128)}) while((s32[]{:T(128)}, bf16[6,512,128]{2,1,0:T(8,128)(2,1)}, bf16[6,512,128]{2,1,0:T(8,128)(2,1)}, bf16[3072,128]{1,0:T(8,128)(2,1)S(1)}, ...), condition=%wide.region_4.5_spmd, body=%wide.region_1.4_spmd.sunk | while | flops 819526656 | bytes 23866464 | solution.py:65
  139.0 2.0 multiply_reduce_fusion.5
  141.0 1.2 fusion.36
  142.2 2.1 fusion.37
  144.2 2.0 multiply_reduce_fusion.5
  146.2 1.2 fusion.36
  147.4 2.1 fusion.37
  149.4 2.0 multiply_reduce_fusion.5
  152.6 2.1 fusion.37
  154.6 2.0 multiply_reduce_fusion.5
  157.8 2.1 fusion.37
  159.8 2.0 multiply_reduce_fusion.5
  161.8 1.2 fusion.36
  163.0 2.1 fusion.37
  165.1 2.0 multiply_reduce_fusion.5
  168.2 2.1 fusion.37
  171.3 4.6 %collective-permute-start.4 = (bf16[1,2,2,2,1,192,1,128]{7,5,4,3,2,1,6,0:T(8,128)(2,1)S(1)}, bf16[1,2,2,2,1,192,1,128]{7,5,4,3,2,1,6,0:T(8,128)(2,1)S(1)}, u32[]{:S(2)}, u32[]{:S(2)}) collective-permute-start(bf16[1,2,2,2,1,192,1,128]{7,5,4,3,2,1,6,0:T(8,128)(2,1)S(1)} %constant_dynamic-slice_fusion.3), channel_id=1, source_target_pairs={{0,4},{4,0},{8,12},{12,8},{16,20},{20,16},{24,28},{28,24},{32,36},... | collective-permute-start | bytes 1179656 | tf_op jit(solution)/shard_map/ppermute | solution.py:14
  175.9 5.4 %collective-permute-done.4 = bf16[1,2,2,2,1,192,1,128]{7,5,4,3,2,1,6,0:T(8,128)(2,1)S(1)} collective-permute-done((bf16[1,2,2,2,1,192,1,128]{7,5,4,3,2,1,6,0:T(8,128)(2,1)S(1)}, bf16[1,2,2,2,1,192,1,128]{7,5,4,3,2,1,6,0:T(8,128)(2,1)S(1)}, u32[]{:S(2)}, u32[]{:S(2)}) %collective-permute-start.4) | collective-permute-done | bytes 393248 | tf_op jit(solution)/shard_map/ppermute | solution.py:14
  183.2 3.2 collective-permute-start.5
  186.3 5.7 %collective-permute-done.5 = bf16[1,2,2,1,2,192,1,128]{7,5,4,3,2,1,6,0:T(8,128)(2,1)S(1)} collective-permute-done((bf16[1,2,2,1,2,192,1,128]{7,5,4,3,2,1,6,0:T(8,128)(2,1)S(1)}, bf16[1,2,2,1,2,192,1,128]{7,5,4,3,2,1,6,0:T(8,128)(2,1)S(1)}, u32[]{:S(2)}, u32[]{:S(2)}) %collective-permute-start.5) | collective-permute-done | bytes 393248 | tf_op jit(solution)/shard_map/ppermute | solution.py:14
  193.9 4.8 %collective-permute-start.6 = (bf16[1,2,1,2,2,192,1,128]{7,5,4,3,2,1,6,0:T(8,128)(2,1)S(1)}, bf16[1,2,1,2,2,192,1,128]{7,5,4,3,2,1,6,0:T(8,128)(2,1)S(1)}, u32[]{:S(2)}, u32[]{:S(2)}) collective-permute-start(bf16[1,2,1,2,2,192,1,128]{7,5,4,3,2,1,6,0:T(8,128)(2,1)S(1)} %constant_dynamic-slice_fusion.1), channel_id=1, source_target_pairs={{0,16},{4,20},{8,24},{12,28},{16,0},{20,4},{24,8},{28,12},{32,48},... | collective-permute-start | bytes 1179656 | tf_op jit(solution)/shard_map/ppermute | solution.py:14
  198.7 5.2 %collective-permute-done.6 = bf16[1,2,1,2,2,192,1,128]{7,5,4,3,2,1,6,0:T(8,128)(2,1)S(1)} collective-permute-done((bf16[1,2,1,2,2,192,1,128]{7,5,4,3,2,1,6,0:T(8,128)(2,1)S(1)}, bf16[1,2,1,2,2,192,1,128]{7,5,4,3,2,1,6,0:T(8,128)(2,1)S(1)}, u32[]{:S(2)}, u32[]{:S(2)}) %collective-permute-start.6) | collective-permute-done | bytes 393248 | tf_op jit(solution)/shard_map/ppermute | solution.py:14
  205.8 3.5 collective-permute-start.7
  210.6 4.2 collective-permute-done.7
  215.6 2.0 multiply_convert_fusion.1
  220.5 109.9 %all-gather.3.cloned.1.call-done = bf16[512,3072]{0,1:T(8,128)(2,1)} async-done(((bf16[512,24]{0,1:T(8,128)(2,1)}), bf16[512,3072]{0,1:T(8,128)(2,1)}) %all-gather.3.cloned.1.call-update) | async-done | bytes 3145744 | tf_op jit(solution)/shard_map/all_gather | solution.py:133
  330.4 3.3 fusion.23
  333.8 1.2 convolution_add_fusion
  335.0 1.4 add_convert_fusion
  336.4 63.0 %all-gather.5.cloned.1.call-done = bf16[4,4,48,3072]{3,2,1,0:T(8,128)(2,1)} async-done(((bf16[1,4,48,3072]{3,2,1,0:T(8,128)(2,1)}), bf16[4,4,48,3072]{3,2,1,0:T(8,128)(2,1)}) %all-gather.5.cloned.1.call-update) | async-done | bytes 4718608 | tf_op jit(solution)/shard_map/all_gather | solution.py:10
  399.4 4.6 %reduce_sum.58 = bf16[4,48,3072]{2,1,0:T(8,128)(2,1)} reduce(bf16[4,4,48,3072]{3,2,1,0:T(8,128)(2,1)} %all-gather.5.cloned.1.call-done, bf16[]{:T(256)} %constant.103.clone.1), dimensions={0}, to_apply=%region_6.7 | reduce | flops 1769472 | bytes 5898242 | tf_op jit(solution)/shard_map/reduce_sum | solution.py:10
  404.0 1.6 multiply_reduce_fusion.2
  405.6 3.4 multiply_reduce_fusion.1
  409.1 2.8 fusion.15
  411.9 8.6 %all_gather.12 = bf16[192,2048]{1,0:T(8,128)(2,1)S(1)} all-gather(bf16[192,512]{1,0:T(8,128)(2,1)S(1)} %fusion.15), channel_id=1, replica_groups=mesh['seq'=128,'branch'=4] {'branch'}, dimensions={1}, use_global_device_ids=true | all-gather | bytes 983040 | tf_op jit(solution)/shard_map/all_gather | solution.py:162
  420.5 1.7 fusion.20
  (80 shorter events, 26.0 us)
Async XLA Ops:
  8.0 322.4 %all-gather.3.cloned.1.call-start = ((), (), s32[]{:S(2)}) async-start(), calls=%async_computation.2 | async-start | bytes 3170304 | tf_op jit(solution)/shard_map/all_gather | solution.py:133
  8.7 1.7 copy-start.6
  13.3 1.3 copy-start.5
  18.6 28.0 %collective-permute-start = (bf16[3,2,2,2,1,192,1,128]{7,5,4,3,2,1,6,0:T(8,128)(2,1)}, bf16[3,2,2,2,1,192,1,128]{7,5,4,3,2,1,6,0:T(8,128)(2,1)S(1)}, u32[]{:S(2)}, u32[]{:S(2)}) collective-permute-start(bf16[3,2,2,2,1,192,1,128]{7,5,4,3,2,1,6,0:T(8,128)(2,1)} %constant_dynamic-slice_fusion.7), channel_id=1, source_target_pairs={{0,4},{4,0},{8,12},{12,8},{16,20},{20,16},{24,28},{28,24},{32,36},... | collective-permute-start | bytes 3538952 | tf_op jit(solution)/shard_map/ppermute | solution.py:14
  47.9 31.3 %collective-permute-start.1 = (bf16[3,2,2,1,2,192,1,128]{7,5,4,3,2,1,6,0:T(8,128)(2,1)}, bf16[3,2,2,1,2,192,1,128]{7,5,4,3,2,1,6,0:T(8,128)(2,1)S(1)}, u32[]{:S(2)}, u32[]{:S(2)}) collective-permute-start(bf16[3,2,2,1,2,192,1,128]{7,5,4,3,2,1,6,0:T(8,128)(2,1)} %constant_dynamic-slice_fusion.6), channel_id=1, source_target_pairs={{0,8},{4,12},{8,0},{12,4},{16,24},{20,28},{24,16},{28,20},{32,40},... | collective-permute-start | bytes 3538952 | tf_op jit(solution)/shard_map/ppermute | solution.py:14
  80.5 28.9 %collective-permute-start.2 = (bf16[3,2,1,2,2,192,1,128]{7,5,4,3,2,1,6,0:T(8,128)(2,1)}, bf16[3,2,1,2,2,192,1,128]{7,5,4,3,2,1,6,0:T(8,128)(2,1)S(1)}, u32[]{:S(2)}, u32[]{:S(2)}) collective-permute-start(bf16[3,2,1,2,2,192,1,128]{7,5,4,3,2,1,6,0:T(8,128)(2,1)} %constant_dynamic-slice_fusion.5), channel_id=1, source_target_pairs={{0,16},{4,20},{8,24},{12,28},{16,0},{20,4},{24,8},{28,12},{32,48},... | collective-permute-start | bytes 3538952 | tf_op jit(solution)/shard_map/ppermute | solution.py:14
  110.8 26.7 %collective-permute-start.3 = (bf16[3,1,2,2,2,192,1,128]{7,5,4,3,2,1,6,0:T(8,128)(2,1)}, bf16[3,1,2,2,2,192,1,128]{7,5,4,3,2,1,6,0:T(8,128)(2,1)S(1)}, u32[]{:S(2)}, u32[]{:S(2)}) collective-permute-start(bf16[3,1,2,2,2,192,1,128]{7,5,4,3,2,1,6,0:T(8,128)(2,1)} %constant_dynamic-slice_fusion.4), channel_id=1, source_target_pairs={{0,32},{4,36},{8,40},{12,44},{16,48},{20,52},{24,56},{28,60},{32,0... | collective-permute-start | bytes 3538952 | tf_op jit(solution)/shard_map/ppermute | solution.py:14
  114.3 216.2 %reduce-scatter.2.cloned.1.call-start = ((), (), s32[]{:S(2)}) async-start(), calls=%async_computation.1 | async-start | bytes 983040 | tf_op jit(solution)/shard_map/reduce_scatter | solution.py:134
  141.0 1.2 copy-start.3
  146.2 1.2 copy-start.3
  151.4 1.2 copy-start.3
  156.6 1.2 copy-start.3
  161.8 1.2 copy-start.3
  167.0 1.2 copy-start.3
  171.3 38.6 %copy-start.9 = (f32[64]{0:T(128)S(1)}, f32[64]{0:T(128)}, u32[]{:S(2)}) copy-start(f32[64]{0:T(128)} %param.17) | copy-start | bytes 772
  171.3 10.0 %collective-permute-start.4 = (bf16[1,2,2,2,1,192,1,128]{7,5,4,3,2,1,6,0:T(8,128)(2,1)S(1)}, bf16[1,2,2,2,1,192,1,128]{7,5,4,3,2,1,6,0:T(8,128)(2,1)S(1)}, u32[]{:S(2)}, u32[]{:S(2)}) collective-permute-start(bf16[1,2,2,2,1,192,1,128]{7,5,4,3,2,1,6,0:T(8,128)(2,1)S(1)} %constant_dynamic-slice_fusion.3), channel_id=1, source_target_pairs={{0,4},{4,0},{8,12},{12,8},{16,20},{20,16},{24,28},{28,24},{32,36},... | collective-permute-start | bytes 1179656 | tf_op jit(solution)/shard_map/ppermute | solution.py:14
  183.2 8.9 %collective-permute-start.5 = (bf16[1,2,2,1,2,192,1,128]{7,5,4,3,2,1,6,0:T(8,128)(2,1)S(1)}, bf16[1,2,2,1,2,192,1,128]{7,5,4,3,2,1,6,0:T(8,128)(2,1)S(1)}, u32[]{:S(2)}, u32[]{:S(2)}) collective-permute-start(bf16[1,2,2,1,2,192,1,128]{7,5,4,3,2,1,6,0:T(8,128)(2,1)S(1)} %constant_dynamic-slice_fusion.2), channel_id=1, source_target_pairs={{0,8},{4,12},{8,0},{12,4},{16,24},{20,28},{24,16},{28,20},{32,40},... | collective-permute-start | bytes 1179656 | tf_op jit(solution)/shard_map/ppermute | solution.py:14
  193.9 10.0 %collective-permute-start.6 = (bf16[1,2,1,2,2,192,1,128]{7,5,4,3,2,1,6,0:T(8,128)(2,1)S(1)}, bf16[1,2,1,2,2,192,1,128]{7,5,4,3,2,1,6,0:T(8,128)(2,1)S(1)}, u32[]{:S(2)}, u32[]{:S(2)}) collective-permute-start(bf16[1,2,1,2,2,192,1,128]{7,5,4,3,2,1,6,0:T(8,128)(2,1)S(1)} %constant_dynamic-slice_fusion.1), channel_id=1, source_target_pairs={{0,16},{4,20},{8,24},{12,28},{16,0},{20,4},{24,8},{28,12},{32,48},... | collective-permute-start | bytes 1179656 | tf_op jit(solution)/shard_map/ppermute | solution.py:14
  205.8 9.1 %collective-permute-start.7 = (bf16[1,1,2,2,2,192,1,128]{7,5,4,3,2,1,6,0:T(8,128)(2,1)S(1)}, bf16[1,1,2,2,2,192,1,128]{7,5,4,3,2,1,6,0:T(8,128)(2,1)S(1)}, u32[]{:S(2)}, u32[]{:S(2)}) collective-permute-start(bf16[1,1,2,2,2,192,1,128]{7,5,4,3,2,1,6,0:T(8,128)(2,1)S(1)} %constant_dynamic-slice_fusion), channel_id=1, source_target_pairs={{0,32},{4,36},{8,40},{12,44},{16,48},{20,52},{24,56},{28,60},{32,0... | collective-permute-start | bytes 1179656 | tf_op jit(solution)/shard_map/ppermute | solution.py:14
  217.7 2.0 copy-start.7
  219.6 179.8 %all-gather.5.cloned.1.call-start = ((), (), s32[]{:S(2)}) async-start(), calls=%async_computation.3 | async-start | bytes 5898240 | tf_op jit(solution)/shard_map/all_gather | solution.py:10
  330.4 3.3 copy-start
  330.4 3.3 copy-start.4
  333.7 1.2 copy-start.2
  336.4 69.2 %copy-start.8 = (f32[3072]{0:T(1024)S(1)}, f32[3072]{0:T(1024)}, u32[]{:S(2)}) copy-start(f32[3072]{0:T(1024)} %param.20) | copy-start | bytes 36868
  411.9 10.3 %copy-start.1 = (f32[192,3072]{1,0:T(8,128)S(1)}, f32[192,3072]{1,0:T(8,128)}, u32[]{:S(2)}) copy-start(f32[192,3072]{1,0:T(8,128)} %get-tuple-element.56) | copy-start | bytes 7077892
Sparse Core Ops, SparseCore 0:
  114.4 215.9 all-gather.2
Sparse Core Ops, SparseCore 1:
  219.7 39.8 reduce-scatter.1
  336.5 62.8 all-gather.4
